TPU v7x, 128 devices: a whole 4x4x4 slice. The times are simulated.
128 devices in a mesh: chaos: 8 (over z, core), space: 16 (over x, y).
Axes of the slice: x: 4, y: 4, z: 4, core: 2. Of those that a mesh axis runs over, the one named last changes fastest.
Arguments:
- panels: bfloat16 [216, 48, 2304], P('chaos', 'space'), may hold values from -6 to 6
- mean_field: float32 [48, 2304], P('space'), may hold values from 0.5 to 2
- fluctuations: float32 [6, 48, 2304], P(None, 'space'), may hold values from -1.5 to 1.5
- products: float32 [1218], replicated, may hold values from -4 to 4
- triples: int32 [1218, 3], replicated, may hold values from 0 to 209, as said below
- owner_slot: int32 [210], replicated, may hold values from 0 to 215, as said below
Outputs:
- first_apply: bfloat16 [216, 48, 2304], P('chaos', 'space')
- second_apply: bfloat16 [216, 48, 2304], P('chaos', 'space')
Inputs may be any that keep to these rules, and one draw needn't show every extreme that they name: `triples`: each row (i, j, k) names a nonzero of G_k; i and j are below 210, k below 7; repeated rows add; every chaos coefficient is some row's i and some row's j. `owner_slot`: distinct slots; slot s belongs to the group s // 27 along chaos.
All inputs are finite; a program needn't handle non-finite values.
Results may differ from a plain program's by a relative error of at most 0.007.
Values may be sent and summed in bfloat16 or wider, within the bound.
A program may use at most 64 MiB of HBM per device.

v0:
```python
import jax
import jax.numpy as jnp
from jax import lax
from jax.sharding import PartitionSpec as P

NXY = 48
scale_factor = 0.15


def padded(block, sides, width):
    for axis, dim in sides:
        count = lax.axis_size(axis)
        forward = [(i, i + 1) for i in range(count - 1)]
        backward = [(target, source) for source, target in forward]
        low = lax.ppermute(
            lax.slice_in_dim(block, block.shape[dim] - width, None, axis=dim), axis, forward
        )
        high = lax.ppermute(lax.slice_in_dim(block, 0, width, axis=dim), axis, backward)
        block = jnp.concatenate([low, block, high], axis=dim)
    return block


def shifted(source, offset, inside):
    length_last = source.shape[-1]
    padding = [(0, 0)] * (source.ndim - 1)
    if offset > 0:
        moved_values = jnp.pad(source[..., offset:], padding + [(0, offset)])
    else:
        moved_values = jnp.pad(source[..., : length_last + offset], padding + [(-offset, 0)])
    return jnp.where(inside, moved_values, jnp.zeros_like(moved_values))


def diffusion(extended, conductance_ext, side_cells):
    center = extended[..., 1:-1, :]
    conduct = conductance_ext[1:-1]
    flux_sum = 0.5 * (conduct + conductance_ext[2:]) * (center - extended[..., 2:, :])
    flux_sum = flux_sum + 0.5 * (conduct + conductance_ext[:-2]) * (center - extended[..., :-2, :])
    column = lax.iota(jnp.int32, center.shape[-1]) % side_cells
    everywhere = column >= 0
    for offset, inside in (
        (1, column < side_cells - 1),
        (-1, column > 0),
        (side_cells, everywhere),
        (-side_cells, everywhere),
    ):
        flux_sum = flux_sum + 0.5 * (conduct + shifted(conduct, offset, inside)) * (
            center - shifted(center, offset, inside)
        )
    return flux_sum


def shards(panels, mean_field, fluctuations, products, triples, owner_slot):
    own_count = panels.shape[0]
    slot_count = own_count * lax.axis_size("chaos")
    coefficients = jnp.concatenate([mean_field[None], fluctuations], axis=0)
    field_count = coefficients.shape[0]
    padded_coef = padded(coefficients, (("space", 1),), 1)
    row_slot = owner_slot[triples[:, 0]]
    column_slot = owner_slot[triples[:, 1]]
    tables = (
        jnp.zeros((field_count, slot_count, slot_count), jnp.float32)
        .at[triples[:, 2], row_slot, column_slot]
        .add(products)
    )
    tables = tables.astype(jnp.bfloat16)
    own_tables = lax.dynamic_slice_in_dim(tables, lax.axis_index("chaos") * own_count, own_count, 1)

    def combine(own_panels):
        summed = jnp.einsum(
            "krc,cpv->krpv",
            own_tables,
            lax.all_gather(own_panels, "chaos", axis=0, tiled=True),
            preferred_element_type=jnp.float32,
        )
        return summed.astype(jnp.bfloat16)

    def galerkin_apply(own_panels):
        combined = padded(combine(own_panels), (("space", 2),), 1)
        combined = lax.optimization_barrier(combined)
        result = jnp.zeros(own_panels.shape, jnp.float32)
        for field_index in range(field_count):
            result = result + diffusion(
                combined[field_index].astype(jnp.float32), padded_coef[field_index], NXY
            )
        return (scale_factor * result).astype(jnp.bfloat16)

    first_values = galerkin_apply(panels)
    second_values = galerkin_apply(first_values)
    return (first_values, second_values)


def solution(mesh):
    in_specs = (P("chaos", "space", None), P("space", None), P(None, "space", None), P(), P(), P())
    out_specs = (P("chaos", "space", None), P("chaos", "space", None))
    return jax.shard_map(shards, mesh=mesh, in_specs=in_specs, out_specs=out_specs, check_vma=False)
```

profile of v0, /device:TPU:6, one launch (start us, length us, event | category | flops | bytes accessed | tf_op | source)
XLA Modules:
  0.0 220.9 jit_solution(4822046470193139959)
XLA Ops:
  8.5 5.2 %collective-permute-start = (f32[7,1,2304]{2,1,0:T(1,128)S(1)}, f32[7,1,2304]{2,1,0:T(1,128)S(1)}, u32[]{:S(2)}, u32[]{:S(2)}) collective-permute-start(f32[7,1,2304]{2,1,0:T(1,128)S(1)} %get-tuple-element.94), channel_id=1, source_target_pairs={{1,0},{2,1},{3,2},{4,3},{5,4},{6,5},{7,6},{8,7},{9,8},{10,9},{11,1... | collective-permute-start | bytes 193544 | tf_op jit(solution)/shard_map/ppermute | solution.py:18
  13.7 1.9 collective-permute-start.3
  15.6 2.1 copy.8
  18.1 8.0 %gather_fusion.1 = s32[1218]{0:T(1024)S(1)} fusion(s32[210]{0:T(256)S(1)} %copy-done, s32[2048]{0:T(1024)S(1)} %get-tuple-element.162), kind=kCustom, calls=%fused_computation.1 | custom fusion | bytes 14616 | tf_op jit(solution)/shard_map/gather | solution.py:59
  26.1 8.0 %gather_fusion = s32[1218]{0:T(1024)S(1)} fusion(s32[210]{0:T(256)S(1)} %copy-done, s32[2048]{0:T(1024)S(1)} %get-tuple-element.163), kind=kCustom, calls=%fused_computation | custom fusion | bytes 14616 | tf_op jit(solution)/shard_map/gather | solution.py:58
  34.3 7.8 %scatter_custom_fusion = f32[326592]{0:T(1024)S(1)} fusion(s32[1218]{0:T(1024)S(1)} %broadcast_select_fusion, f32[1218]{0:T(1024)} %param.9, f32[]{:T(128)} %constant.69.clone.1), kind=kCustom, calls=%fused_computation.181 | custom fusion | flops 1218 | bytes 1306880
  42.2 2.5 %reshape.112 = bf16[7,216,216]{2,1,0:T(8,128)(2,1)S(1)} reshape(bf16[326592]{0:T(1024)(128)(2,1)S(1)} %convert_element_type.252) | data formatting | bytes 1306368 | tf_op jit(solution)/shard_map/convert_element_type | solution.py:65
  49.5 2.7 %all-gather.3.cloned.1.call-done = bf16[216,3,2304]{2,1,0:T(4,128)(2,1)} async-done(((bf16[27,3,2304]{2,1,0:T(4,128)(2,1)}), bf16[216,3,2304]{2,1,0:T(4,128)(2,1)}) %all-gather.3.cloned.1.call-update) | async-done | bytes 2986000 | tf_op jit(solution)/shard_map/all_gather | solution.py:72
  52.2 3.1 %convolution_convert_fusion.1 = bf16[7,27,3,2304]{3,1,2,0:T(8,128)(2,1)S(1)} fusion(bf16[216,3,2304]{2,1,0:T(4,128)(2,1)} %all-gather.3.cloned.1.call-done, bf16[7,216,216]{2,1,0:T(8,128)(2,1)S(1)} %reshape.112, s32[]{:T(128)S(6)} %select_n.521), kind=kOutput, calls=%fused_computation.6 | convolution fusion | flops 565657344 | bytes 5713412 | tf_op jit(solution)/shard_map/krc,cpv->krpv/dot_general | solution.py:69
  56.6 4.9 %collective-permute-start.2 = (bf16[7,27,1,2304]{3,0,2,1:T(8,128)(2,1)S(1)}, bf16[7,27,1,2304]{3,0,2,1:T(8,128)(2,1)S(1)}, u32[]{:S(2)}, u32[]{:S(2)}) collective-permute-start(bf16[7,27,1,2304]{3,0,2,1:T(8,128)(2,1)S(1)} %copy.11), channel_id=1, source_target_pairs={{1,0},{2,1},{3,2},{4,3},{5,4},{6,5},{7,6},{8,7},{9,8},{10,9},{11,1... | collective-permute-start | bytes 2612744 | tf_op jit(solution)/shard_map/ppermute | solution.py:18
  61.5 2.1 collective-permute-start.1
  64.6 18.6 %collective-permute-done.2 = bf16[7,27,1,2304]{3,0,2,1:T(8,128)(2,1)S(1)} collective-permute-done((bf16[7,27,1,2304]{3,0,2,1:T(8,128)(2,1)S(1)}, bf16[7,27,1,2304]{3,0,2,1:T(8,128)(2,1)S(1)}, u32[]{:S(2)}, u32[]{:S(2)}) %collective-permute-start.2) | collective-permute-done | bytes 870944 | tf_op jit(solution)/shard_map/ppermute | solution.py:18
  83.3 6.1 %collective-permute-done.1 = bf16[7,27,1,2304]{3,0,2,1:T(8,128)(2,1)S(1)} collective-permute-done((bf16[7,27,1,2304]{3,0,2,1:T(8,128)(2,1)S(1)}, bf16[7,27,1,2304]{3,0,2,1:T(8,128)(2,1)S(1)}, u32[]{:S(2)}, u32[]{:S(2)}) %collective-permute-start.1) | collective-permute-done | bytes 870944 | tf_op jit(solution)/shard_map/ppermute | solution.py:15
  100.9 1.6 fusion.197
  105.5 12.3 %fusion.69 = bf16[27,3,2304]{2,0,1:T(8,128)(2,1)} fusion(f32[27,5,2304]{2,0,1:T(8,128)S(1)} %get-tuple-element.12, f32[27,5,2304]{2,0,1:T(8,128)S(1)} %get-tuple-element.13, f32[27,5,2304]{2,0,1:T(8,128)S(1)} %get-tuple-element.14, f32[27,5,2304]{2,0,1:T(8,128)S(1)} %get-tuple-element.15, f32[27,5,2304]{2,0,1:T(8,128)S(1)} %get-tuple-element.16, ...), kind=kLoop, calls=%fused_computation.91 | loop fusion | flops 28926720 | bytes 37897416 | tf_op jit(solution)/shard_map/convert_element_type | solution.py:85
  117.8 2.1 copy.14
  119.9 28.6 %all-gather.5.cloned.1.call-done = bf16[216,3,2304]{2,1,0:T(4,128)(2,1)} async-done(((bf16[27,3,2304]{2,1,0:T(4,128)(2,1)}), bf16[216,3,2304]{2,1,0:T(4,128)(2,1)}) %all-gather.5.cloned.1.call-update) | async-done | bytes 2986000 | tf_op jit(solution)/shard_map/all_gather | solution.py:72
  148.5 3.2 %convolution_convert_fusion = bf16[7,27,3,2304]{3,1,2,0:T(8,128)(2,1)S(1)} fusion(bf16[216,3,2304]{2,1,0:T(4,128)(2,1)} %all-gather.5.cloned.1.call-done, bf16[7,216,216]{2,1,0:T(8,128)(2,1)} %copy-done.4, s32[]{:T(128)S(6)} %select_n.521), kind=kOutput, calls=%fused_computation.5 | convolution fusion | flops 565657344 | bytes 6708740 | tf_op jit(solution)/shard_map/krc,cpv->krpv/dot_general | solution.py:69
  152.4 4.9 %collective-permute-start.5 = (bf16[7,27,1,2304]{3,0,2,1:T(8,128)(2,1)S(1)}, bf16[7,27,1,2304]{3,0,2,1:T(8,128)(2,1)S(1)}, u32[]{:S(2)}, u32[]{:S(2)}) collective-permute-start(bf16[7,27,1,2304]{3,0,2,1:T(8,128)(2,1)S(1)} %copy.17), channel_id=1, source_target_pairs={{1,0},{2,1},{3,2},{4,3},{5,4},{6,5},{7,6},{8,7},{9,8},{10,9},{11,1... | collective-permute-start | bytes 2612744 | tf_op jit(solution)/shard_map/ppermute | solution.py:18
  157.8 2.1 collective-permute-start.4
  160.0 19.0 %collective-permute-done.5 = bf16[7,27,1,2304]{3,0,2,1:T(8,128)(2,1)S(1)} collective-permute-done((bf16[7,27,1,2304]{3,0,2,1:T(8,128)(2,1)S(1)}, bf16[7,27,1,2304]{3,0,2,1:T(8,128)(2,1)S(1)}, u32[]{:S(2)}, u32[]{:S(2)}) %collective-permute-start.5) | collective-permute-done | bytes 870944 | tf_op jit(solution)/shard_map/ppermute | solution.py:18
  179.1 6.6 %collective-permute-done.4 = bf16[7,27,1,2304]{3,0,2,1:T(8,128)(2,1)S(1)} collective-permute-done((bf16[7,27,1,2304]{3,0,2,1:T(8,128)(2,1)S(1)}, bf16[7,27,1,2304]{3,0,2,1:T(8,128)(2,1)S(1)}, u32[]{:S(2)}, u32[]{:S(2)}) %collective-permute-start.4) | collective-permute-done | bytes 870944 | tf_op jit(solution)/shard_map/ppermute | solution.py:15
  197.2 1.6 fusion.183
  201.8 12.3 %fusion.12 = bf16[27,3,2304]{2,0,1:T(8,128)(2,1)} fusion(f32[27,5,2304]{2,0,1:T(8,128)S(1)} %get-tuple-element.5, f32[27,5,2304]{2,0,1:T(8,128)S(1)} %get-tuple-element.6, f32[27,5,2304]{2,0,1:T(8,128)S(1)} %get-tuple-element.7, f32[27,5,2304]{2,0,1:T(8,128)S(1)} %get-tuple-element.8, f32[27,5,2304]{2,0,1:T(8,128)S(1)} %get-tuple-element.9, ...), kind=kLoop, calls=%fused_computation.20 | loop fusion | flops 28926720 | bytes 37897416 | tf_op jit(solution)/shard_map/convert_element_type | solution.py:85
  (88 shorter events, 39.1 us)
Async XLA Ops:
  7.2 10.9 %copy-start = (s32[210]{0:T(256)S(1)}, s32[210]{0:T(256)}, u32[]{:S(2)}) copy-start(s32[210]{0:T(256)} %param.11) | copy-start | bytes 2524
  7.2 10.6 %copy-start.3 = (f32[3,2304]{1,0:T(4,128)S(1)}, f32[3,2304]{1,0:T(4,128)}, u32[]{:S(2)}) copy-start(f32[3,2304]{1,0:T(4,128)} %param.7) | copy-start | bytes 82948
  7.2 10.8 %copy-start.5 = (s32[1218,3]{0,1:T(4,128)S(1)}, s32[1218,3]{0,1:T(4,128)}, u32[]{:S(2)}) copy-start(s32[1218,3]{0,1:T(4,128)} %param.10) | copy-start | bytes 43852
  7.2 45.0 %all-gather.3.cloned.1.call-start = ((), (), s32[]{:S(2)}) async-start(), calls=%async_computation | async-start | bytes 4478976 | tf_op jit(solution)/shard_map/all_gather | solution.py:72
  8.5 36.3 %collective-permute-start = (f32[7,1,2304]{2,1,0:T(1,128)S(1)}, f32[7,1,2304]{2,1,0:T(1,128)S(1)}, u32[]{:S(2)}, u32[]{:S(2)}) collective-permute-start(f32[7,1,2304]{2,1,0:T(1,128)S(1)} %get-tuple-element.94), channel_id=1, source_target_pairs={{1,0},{2,1},{3,2},{4,3},{5,4},{6,5},{7,6},{8,7},{9,8},{10,9},{11,1... | collective-permute-start | bytes 193544 | tf_op jit(solution)/shard_map/ppermute | solution.py:18
  13.7 31.1 %collective-permute-start.3 = (f32[7,1,2304]{2,1,0:T(1,128)S(1)}, f32[7,1,2304]{2,1,0:T(1,128)S(1)}, u32[]{:S(2)}, u32[]{:S(2)}) collective-permute-start(f32[7,1,2304]{2,1,0:T(1,128)S(1)} %get-tuple-element.95), channel_id=1, source_target_pairs={{0,1},{1,2},{2,3},{3,4},{4,5},{5,6},{6,7},{7,8},{8,9},{9,10},{10,1... | collective-permute-start | bytes 193544 | tf_op jit(solution)/shard_map/ppermute | solution.py:15
  17.7 130.7 %all-gather.5.cloned.1.call-start = ((), (), s32[]{:S(2)}) async-start(), calls=%async_computation.1 | async-start | bytes 4478976 | tf_op jit(solution)/shard_map/all_gather | solution.py:72
  26.1 8.0 %copy-start.7 = (s32[3]{0:T(128)S(1)}, s32[3]{0:T(128)}, u32[]{:S(2)}) copy-start(s32[3]{0:T(128)} %constant.254) | copy-start | bytes 40
  26.1 8.1 %copy-start.6 = (s32[3]{0:T(128)S(1)}, s32[3]{0:T(128)}, u32[]{:S(2)}) copy-start(s32[3]{0:T(128)} %constant.251) | copy-start | bytes 40
  42.1 2.7 %copy-start.2 = (f32[6,3,2304]{2,1,0:T(4,128)S(1)}, f32[6,3,2304]{2,1,0:T(4,128)}, u32[]{:S(2)}) copy-start(f32[6,3,2304]{2,1,0:T(4,128)} %param.8) | copy-start | bytes 497668
  44.7 7.5 %copy-start.4 = (bf16[7,216,216]{2,1,0:T(8,128)(2,1)}, bf16[7,216,216]{2,1,0:T(8,128)(2,1)S(1)}, u32[]{:S(2)}) copy-start(bf16[7,216,216]{2,1,0:T(8,128)(2,1)S(1)} %reshape.112) | copy-start | bytes 1959556
  56.6 26.6 %collective-permute-start.2 = (bf16[7,27,1,2304]{3,0,2,1:T(8,128)(2,1)S(1)}, bf16[7,27,1,2304]{3,0,2,1:T(8,128)(2,1)S(1)}, u32[]{:S(2)}, u32[]{:S(2)}) collective-permute-start(bf16[7,27,1,2304]{3,0,2,1:T(8,128)(2,1)S(1)} %copy.11), channel_id=1, source_target_pairs={{1,0},{2,1},{3,2},{4,3},{5,4},{6,5},{7,6},{8,7},{9,8},{10,9},{11,1... | collective-permute-start | bytes 2612744 | tf_op jit(solution)/shard_map/ppermute | solution.py:18
  61.5 27.9 %collective-permute-start.1 = (bf16[7,27,1,2304]{3,0,2,1:T(8,128)(2,1)S(1)}, bf16[7,27,1,2304]{3,0,2,1:T(8,128)(2,1)S(1)}, u32[]{:S(2)}, u32[]{:S(2)}) collective-permute-start(bf16[7,27,1,2304]{3,0,2,1:T(8,128)(2,1)S(1)} %copy.10), channel_id=1, source_target_pairs={{0,1},{1,2},{2,3},{3,4},{4,5},{5,6},{6,7},{7,8},{8,9},{9,10},{10,1... | collective-permute-start | bytes 2612744 | tf_op jit(solution)/shard_map/ppermute | solution.py:15
  152.4 26.6 %collective-permute-start.5 = (bf16[7,27,1,2304]{3,0,2,1:T(8,128)(2,1)S(1)}, bf16[7,27,1,2304]{3,0,2,1:T(8,128)(2,1)S(1)}, u32[]{:S(2)}, u32[]{:S(2)}) collective-permute-start(bf16[7,27,1,2304]{3,0,2,1:T(8,128)(2,1)S(1)} %copy.17), channel_id=1, source_target_pairs={{1,0},{2,1},{3,2},{4,3},{5,4},{6,5},{7,6},{8,7},{9,8},{10,9},{11,1... | collective-permute-start | bytes 2612744 | tf_op jit(solution)/shard_map/ppermute | solution.py:18
  157.8 27.9 %collective-permute-start.4 = (bf16[7,27,1,2304]{3,0,2,1:T(8,128)(2,1)S(1)}, bf16[7,27,1,2304]{3,0,2,1:T(8,128)(2,1)S(1)}, u32[]{:S(2)}, u32[]{:S(2)}) collective-permute-start(bf16[7,27,1,2304]{3,0,2,1:T(8,128)(2,1)S(1)} %copy.16), channel_id=1, source_target_pairs={{0,1},{1,2},{2,3},{3,4},{4,5},{5,6},{6,7},{7,8},{8,9},{9,10},{10,1... | collective-permute-start | bytes 2612744 | tf_op jit(solution)/shard_map/ppermute | solution.py:15
  201.8 12.3 %copy-start.1 = (s32[210]{0:T(256)S(1)}, s32[210]{0:T(256)}, u32[]{:S(2)}) copy-start(s32[210]{0:T(256)} %param.11) | copy-start | bytes 2524
Sparse Core Ops, SparseCore 0:
  17.8 34.3 all-gather.2
  120.0 28.4 all-gather.4
where the time goes:
time: 221 us
  waiting for transfers between devices  81.5 us (37%)
  local copies, waits for them, and re-layouts  54.2 us (25%)
  other arithmetic  43 us (19%)
  starting transfers between devices  21.3 us (10%)
  between operations  14.5 us (7%)
  matrix products  6.38 us (3%)
    ppermute x3, waiting for transfers between devices, padded(): lax.ppermute(lax.slice_in_dim(block, 0, width, axis=dim), axis, backward)  37.6 us
    all_gather x2, waiting for transfers between devices, combine(): lax.all_gather(own_panels, 'chaos', axis=0, tiled=True)  31.3 us
    slice x36, local copies, waits for them, and re-layouts, shifted(): moved_values = jnp.pad(source[..., offset:], padding + [(0, offset)])  28.5 us
    convert_element_type x2, other arithmetic, galerkin_apply(): return (scale_factor * result).astype(jnp.bfloat16)  24.6 us
    ppermute x3, starting transfers between devices, padded(): lax.ppermute(lax.slice_in_dim(block, 0, width, axis=dim), axis, backward)  15.1 us
    ppermute x3, waiting for transfers between devices, padded(): lax.ppermute(lax.slice_in_dim(block, block.shape[dim] - width, None, axis...  12.6 us
    gather x1, local copies, waits for them, and re-layouts, shards(): column_slot = owner_slot[triples[:, 1]]  7.98 us
    gather x1, local copies, waits for them, and re-layouts, shards(): row_slot = owner_slot[triples[:, 0]]  7.98 us
  transfers between devices with their start and end apart: 8, of which 6 were waited for; matrix products, arithmetic and copies ran while one was open for 16% of the time, Pallas kernels for 0%

commit v1 on v0

--- a/solution.py
+++ b/solution.py
@@ -66,10 +66,19 @@
     own_tables = lax.dynamic_slice_in_dim(tables, lax.axis_index("chaos") * own_count, own_count, 1)
 
     def combine(own_panels):
+        group_the_packet = lambda mat: jnp.concatenate(
+            lax.all_to_all(
+                jnp.stack([mat] * lax.axis_size("chaos"), axis=0),
+                axis_name="chaos",
+                split_axis=0,
+                concat_axis=0,
+            ),
+            axis=0,
+        )
         summed = jnp.einsum(
             "krc,cpv->krpv",
             own_tables,
-            lax.all_gather(own_panels, "chaos", axis=0, tiled=True),
+            group_the_packet(own_panels),
             preferred_element_type=jnp.float32,
         )
         return summed.astype(jnp.bfloat16)

time: 221 us -> 258 us (1.17)
  blocking collectives: 0 us -> 46.9 us
  waiting for transfers between devices: 81.5 us -> 48 us
  local copies, waits for them, and re-layouts: 54.2 us -> 74.6 us
  between operations: 14.5 us -> 1.28 us
  other arithmetic: 43 us -> 54.6 us
  starting transfers between devices: 21.3 us -> 26.6 us
    all_to_all x0 -> x1, blocking collectives: none -> 46.9 us  [combine(): lax.all_to_all(jnp.stack([mat] * lax.axis_size('chaos'), axis=0), axis_na...]
    all_gather x2 -> x0, waiting for transfers between devices: 31.3 us -> none  [combine(): lax.all_gather(own_panels, 'chaos', axis=0, tiled=True)]
    reshape x0 -> x2, local copies, waits for them, and re-layouts: none -> 5.88 us  [combine(): jnp.concatenate(lax.all_to_all(jnp.stack([mat] * lax.axis_size('chaos'),...]
    all_to_all x0 -> x1, starting transfers between devices: none -> 5.31 us  [combine(): lax.all_to_all(jnp.stack([mat] * lax.axis_size('chaos'), axis=0), axis_na...]
    another operation x0 -> x2, local copies, waits for them, and re-layouts: none -> 4.53 us  [combine(): jnp.stack([mat] * lax.axis_size('chaos'), axis=0)]
    slice x36, local copies, waits for them, and re-layouts: 28.5 us -> 32.7 us  [shifted(): moved_values = jnp.pad(source[..., offset:], padding + [(0, offset)])]
    gather x1, local copies, waits for them, and re-layouts: 7.98 us -> 11.1 us  [shards(): row_slot = owner_slot[triples[:, 0]]]
    gather x1, local copies, waits for them, and re-layouts: 7.98 us -> 10.9 us  [shards(): column_slot = owner_slot[triples[:, 1]]]
  transfers between devices with their start and end apart: 8 -> 7, of which waited for: 6 -> 4; matrix products, arithmetic and copies ran while one was open for 16% -> 23% of each run, Pallas kernels for 0% -> 0%
where the time goes in v1:
time: 258 us; the launch traced here: 257 us
  local copies, waits for them, and re-layouts  74.6 us (29%)
  other arithmetic  54.6 us (21%)
  waiting for transfers between devices  48 us (19%)
  blocking collectives  46.9 us (18%)
  starting transfers between devices  26.6 us (10%)
  matrix products  4.79 us (2%)
    all_to_all x1, blocking collectives, combine(): lax.all_to_all(jnp.stack([mat] * lax.axis_size('chaos'), axis=0), axis_na...  46.9 us
    ppermute x3, waiting for transfers between devices, padded(): lax.ppermute(lax.slice_in_dim(block, 0, width, axis=dim), axis, backward)  37.6 us
    slice x36, local copies, waits for them, and re-layouts, shifted(): moved_values = jnp.pad(source[..., offset:], padding + [(0, offset)])  32.7 us
    convert_element_type x2, other arithmetic, galerkin_apply(): return (scale_factor * result).astype(jnp.bfloat16)  24.5 us
    ppermute x3, starting transfers between devices, padded(): lax.ppermute(lax.slice_in_dim(block, 0, width, axis=dim), axis, backward)  13.1 us
    gather x1, local copies, waits for them, and re-layouts, shards(): row_slot = owner_slot[triples[:, 0]]  11.1 us
    gather x1, local copies, waits for them, and re-layouts, shards(): column_slot = owner_slot[triples[:, 1]]  10.9 us
    unnamed x4, other arithmetic  10.8 us
  transfers between devices with their start and end apart: 7, of which 4 were waited for; matrix products, arithmetic and copies ran while one was open for 23% of the time, Pallas kernels for 0%

profile of v1, /device:TPU:6, one launch (start us, length us, event | category | flops | bytes accessed | tf_op | source)
XLA Modules:
  0.0 256.8 jit_solution(1679194752362369505)
XLA Ops:
  2.5 5.2 %collective-permute-start = (f32[7,1,2304]{2,1,0:T(1,128)}, f32[7,1,2304]{2,1,0:T(1,128)}, u32[]{:S(2)}, u32[]{:S(2)}) collective-permute-start(f32[7,1,2304]{2,1,0:T(1,128)} %get-tuple-element.94), channel_id=1, source_target_pairs={{1,0},{2,1},{3,2},{4,3},{5,4},{6,5},{7,6},{8,7},{9,8},{10,9},{11,1... | collective-permute-start | bytes 193544 | tf_op jit(solution)/shard_map/ppermute | solution.py:18
  7.7 1.9 collective-permute-start.3
  9.6 3.1 %stack.4 = bf16[8,27,3,2304]{3,1,2,0:T(8,128)(2,1)} broadcast(bf16[27,3,2304]{2,0,1:T(8,128)(2,1)} %param.6), dimensions={1,2,3} | broadcast | bytes 3359232 | tf_op jit(solution)/shard_map/stack | solution.py:71
  12.8 5.3 %all-to-all-start = ((bf16[8,27,3,2304]{3,1,2,0:T(8,128)(2,1)}), bf16[8,27,3,2304]{3,1,2,0:T(8,128)(2,1)S(1)}, u32[]{:S(2)}, u32[]{:S(2)}) async-start(bf16[8,27,3,2304]{3,1,2,0:T(8,128)(2,1)} %stack.4), calls=%async_computation | async-start | bytes 7077888 | tf_op jit(solution)/shard_map/all_to_all | solution.py:70
  23.2 10.9 %gather_fusion.1 = s32[1218]{0:T(1024)} fusion(s32[210]{0:T(256)S(1)} %copy-done, s32[2048]{0:T(1024)} %get-tuple-element.162), kind=kCustom, calls=%fused_computation.1 | custom fusion | bytes 14616 | tf_op jit(solution)/shard_map/gather | solution.py:59
  35.5 11.1 %gather_fusion = s32[1218]{0:T(1024)} fusion(s32[210]{0:T(256)S(1)} %copy-done, s32[2048]{0:T(1024)} %get-tuple-element.163), kind=kCustom, calls=%fused_computation | custom fusion | bytes 14616 | tf_op jit(solution)/shard_map/gather | solution.py:58
  49.4 8.5 %scatter_custom_fusion = f32[326592]{0:T(1024)} fusion(s32[1218]{0:T(1024)} %broadcast_select_fusion, f32[1218]{0:T(1024)} %param.9, f32[]{:T(128)} %constant.69.clone.1), kind=kCustom, calls=%fused_computation.177 | custom fusion | flops 1218 | bytes 1306880
  58.0 2.2 convert_element_type.252
  60.2 4.2 %reshape.124 = bf16[7,216,216]{2,1,0:T(8,128)(2,1)} reshape(bf16[326592]{0:T(1024)(128)(2,1)} %convert_element_type.252) | data formatting | bytes 1306368 | tf_op jit(solution)/shard_map/convert_element_type | solution.py:65
  72.6 2.0 copy.8
  74.7 3.2 %reshape.162 = bf16[216,3,2304,1]{2,0,1,3:T(8,128)(2,1)S(1)} reshape(bf16[8,27,3,2304]{3,1,0,2:T(8,128)(2,1)} %copy.8) | data formatting | bytes 5971968 | tf_op jit(solution)/shard_map/reshape | solution.py:69
  81.1 6.0 %collective-permute-start.2 = (bf16[7,27,1,2304]{3,0,2,1:T(8,128)(2,1)S(1)}, bf16[7,27,1,2304]{3,0,2,1:T(8,128)(2,1)S(1)}, u32[]{:S(2)}, u32[]{:S(2)}) collective-permute-start(bf16[7,27,1,2304]{3,0,2,1:T(8,128)(2,1)S(1)} %copy.10), channel_id=1, source_target_pairs={{1,0},{2,1},{3,2},{4,3},{5,4},{6,5},{7,6},{8,7},{9,8},{10,9},{11,1... | collective-permute-start | bytes 2612744 | tf_op jit(solution)/shard_map/ppermute | solution.py:18
  87.1 2.1 collective-permute-start.1
  90.3 18.7 %collective-permute-done.2 = bf16[7,27,1,2304]{3,0,2,1:T(8,128)(2,1)S(1)} collective-permute-done((bf16[7,27,1,2304]{3,0,2,1:T(8,128)(2,1)S(1)}, bf16[7,27,1,2304]{3,0,2,1:T(8,128)(2,1)S(1)}, u32[]{:S(2)}, u32[]{:S(2)}) %collective-permute-start.2) | collective-permute-done | bytes 870944 | tf_op jit(solution)/shard_map/ppermute | solution.py:18
  109.2 6.1 %collective-permute-done.1 = bf16[7,27,1,2304]{3,0,2,1:T(8,128)(2,1)S(1)} collective-permute-done((bf16[7,27,1,2304]{3,0,2,1:T(8,128)(2,1)S(1)}, bf16[7,27,1,2304]{3,0,2,1:T(8,128)(2,1)S(1)}, u32[]{:S(2)}, u32[]{:S(2)}) %collective-permute-start.1) | collective-permute-done | bytes 870944 | tf_op jit(solution)/shard_map/ppermute | solution.py:15
  131.3 12.2 %fusion.65 = bf16[27,3,2304]{2,0,1:T(8,128)(2,1)} fusion(f32[27,5,2304]{2,0,1:T(8,128)S(1)} %get-tuple-element.12, f32[27,5,2304]{2,0,1:T(8,128)S(1)} %get-tuple-element.13, f32[27,5,2304]{2,0,1:T(8,128)S(1)} %get-tuple-element.14, f32[27,5,2304]{2,0,1:T(8,128)S(1)} %get-tuple-element.15, f32[27,5,2304]{2,0,1:T(8,128)S(1)} %get-tuple-element.16, ...), kind=kLoop, calls=%fused_computation.87 | loop fusion | flops 28926720 | bytes 37897416 | tf_op jit(solution)/shard_map/convert_element_type | solution.py:94
  145.0 46.9 %all_to_all.10 = bf16[8,27,3,2304]{3,1,2,0:T(8,128)(2,1)S(1)} all-to-all(bf16[8,27,3,2304]{3,1,2,0:T(8,128)(2,1)S(1)} %stack.5), channel_id=1, replica_groups=mesh['chaos'=8,'space'=16] {'chaos'}, dimensions={0} | all-to-all | bytes 5971968 | tf_op jit(solution)/shard_map/all_to_all | solution.py:70
  192.1 2.7 %reshape.163 = bf16[216,3,2304,1]{2,0,1,3:T(8,128)(2,1)} reshape(bf16[8,27,3,2304]{3,1,0,2:T(8,128)(2,1)S(1)} %copy.13) | data formatting | bytes 5971968 | tf_op jit(solution)/shard_map/reshape | solution.py:69
  194.8 2.9 %convolution_convert_fusion = bf16[7,27,3,2304]{3,1,2,0:T(8,128)(2,1)S(1)} fusion(bf16[216,3,2304,1]{2,0,1,3:T(8,128)(2,1)} %reshape.163, bf16[7,216,216]{2,1,0:T(8,128)(2,1)} %reshape.124, s32[]{:T(128)S(6)} %select_n.521), kind=kOutput, calls=%fused_computation.5 | convolution fusion | flops 565657344 | bytes 5713412 | tf_op jit(solution)/shard_map/krc,cpv->krpv/dot_general | solution.py:78
  198.3 1.9 collective-permute-start.5
  200.7 4.1 %collective-permute-start.4 = (bf16[7,27,1,2304]{3,0,2,1:T(8,128)(2,1)S(1)}, bf16[7,27,1,2304]{3,0,2,1:T(8,128)(2,1)S(1)}, u32[]{:S(2)}, u32[]{:S(2)}) collective-permute-start(bf16[7,27,1,2304]{3,0,2,1:T(8,128)(2,1)S(1)} %copy.14), channel_id=1, source_target_pairs={{0,1},{1,2},{2,3},{3,4},{4,5},{5,6},{6,7},{7,8},{8,9},{9,10},{10,1... | collective-permute-start | bytes 2612744 | tf_op jit(solution)/shard_map/ppermute | solution.py:15
  204.9 18.9 %collective-permute-done.5 = bf16[7,27,1,2304]{3,0,2,1:T(8,128)(2,1)S(1)} collective-permute-done((bf16[7,27,1,2304]{3,0,2,1:T(8,128)(2,1)S(1)}, bf16[7,27,1,2304]{3,0,2,1:T(8,128)(2,1)S(1)}, u32[]{:S(2)}, u32[]{:S(2)}) %collective-permute-start.5) | collective-permute-done | bytes 870944 | tf_op jit(solution)/shard_map/ppermute | solution.py:18
  223.9 4.4 %collective-permute-done.4 = bf16[7,27,1,2304]{3,0,2,1:T(8,128)(2,1)S(1)} collective-permute-done((bf16[7,27,1,2304]{3,0,2,1:T(8,128)(2,1)S(1)}, bf16[7,27,1,2304]{3,0,2,1:T(8,128)(2,1)S(1)}, u32[]{:S(2)}, u32[]{:S(2)}) %collective-permute-start.4) | collective-permute-done | bytes 870944 | tf_op jit(solution)/shard_map/ppermute | solution.py:15
  244.4 12.2 %fusion.8 = bf16[27,3,2304]{2,0,1:T(8,128)(2,1)} fusion(f32[27,5,2304]{2,0,1:T(8,128)S(1)} %get-tuple-element.5, f32[27,5,2304]{2,0,1:T(8,128)S(1)} %get-tuple-element.6, f32[27,5,2304]{2,0,1:T(8,128)S(1)} %get-tuple-element.7, f32[27,5,2304]{2,0,1:T(8,128)S(1)} %get-tuple-element.8, f32[27,5,2304]{2,0,1:T(8,128)S(1)} %get-tuple-element.9, ...), kind=kLoop, calls=%fused_computation.16 | loop fusion | flops 28926720 | bytes 37897416 | tf_op jit(solution)/shard_map/convert_element_type | solution.py:94
  (115 shorter events, 58.7 us)
Async XLA Ops:
  0.6 22.6 %copy-start = (s32[210]{0:T(256)S(1)}, s32[210]{0:T(256)}, u32[]{:S(2)}) copy-start(s32[210]{0:T(256)} %param.11) | copy-start | bytes 2524
  2.5 62.0 %collective-permute-start = (f32[7,1,2304]{2,1,0:T(1,128)}, f32[7,1,2304]{2,1,0:T(1,128)}, u32[]{:S(2)}, u32[]{:S(2)}) collective-permute-start(f32[7,1,2304]{2,1,0:T(1,128)} %get-tuple-element.94), channel_id=1, source_target_pairs={{1,0},{2,1},{3,2},{4,3},{5,4},{6,5},{7,6},{8,7},{9,8},{10,9},{11,1... | collective-permute-start | bytes 193544 | tf_op jit(solution)/shard_map/ppermute | solution.py:18
  7.7 56.8 %collective-permute-start.3 = (f32[7,1,2304]{2,1,0:T(1,128)}, f32[7,1,2304]{2,1,0:T(1,128)}, u32[]{:S(2)}, u32[]{:S(2)}) collective-permute-start(f32[7,1,2304]{2,1,0:T(1,128)} %get-tuple-element.95), channel_id=1, source_target_pairs={{0,1},{1,2},{2,3},{3,4},{4,5},{5,6},{6,7},{7,8},{8,9},{9,10},{10,1... | collective-permute-start | bytes 193544 | tf_op jit(solution)/shard_map/ppermute | solution.py:15
  12.8 59.9 %all-to-all-start = ((bf16[8,27,3,2304]{3,1,2,0:T(8,128)(2,1)}), bf16[8,27,3,2304]{3,1,2,0:T(8,128)(2,1)S(1)}, u32[]{:S(2)}, u32[]{:S(2)}) async-start(bf16[8,27,3,2304]{3,1,2,0:T(8,128)(2,1)} %stack.4), calls=%async_computation | async-start | bytes 7077888 | tf_op jit(solution)/shard_map/all_to_all | solution.py:70
  35.5 12.6 %copy-start.20 = (s32[3]{0:T(128)S(1)}, s32[3]{0:T(128)}, u32[]{:S(2)}) copy-start(s32[3]{0:T(128)} %constant.251) | copy-start | bytes 40
  64.4 4.0 %copy-start.2 = (f32[6,3,2304]{2,1,0:T(4,128)S(1)}, f32[6,3,2304]{2,1,0:T(4,128)}, u32[]{:S(2)}) copy-start(f32[6,3,2304]{2,1,0:T(4,128)} %param.8) | copy-start | bytes 497668
  64.4 4.0 %copy-start.4 = (f32[3,2304]{1,0:T(4,128)S(1)}, f32[3,2304]{1,0:T(4,128)}, u32[]{:S(2)}) copy-start(f32[3,2304]{1,0:T(4,128)} %param.7) | copy-start | bytes 82948
  67.5 3.4 %copy-start.5 = (f32[3,2304]{1,0:T(4,128)}, f32[3,2304]{1,0:T(4,128)S(1)}, u32[]{:S(2)}) copy-start(f32[3,2304]{1,0:T(4,128)S(1)} %get-tuple-element.122) | copy-start | bytes 82948
  67.6 3.4 %copy-start.7 = (f32[3,2304]{1,0:T(4,128)}, f32[3,2304]{1,0:T(4,128)S(1)}, u32[]{:S(2)}) copy-start(f32[3,2304]{1,0:T(4,128)S(1)} %get-tuple-element.123) | copy-start | bytes 82948
  68.4 3.4 %copy-start.11 = (f32[3,2303]{1,0:T(4,128)S(1)}, f32[3,2303]{1,0:T(4,128)}, u32[]{:S(2)}) copy-start(f32[3,2303]{1,0:T(4,128)} %get-tuple-element.129) | copy-start | bytes 82912
  68.4 3.4 %copy-start.12 = (f32[3,2303]{1,0:T(4,128)S(1)}, f32[3,2303]{1,0:T(4,128)}, u32[]{:S(2)}) copy-start(f32[3,2303]{1,0:T(4,128)} %get-tuple-element.130) | copy-start | bytes 82912
  80.5 8.7 %copy-start.6 = (f32[3,2304]{1,0:T(4,128)S(1)}, f32[3,2304]{1,0:T(4,128)}, u32[]{:S(2)}) copy-start(f32[3,2304]{1,0:T(4,128)} %copy-done.5) | copy-start | bytes 82948
  80.5 8.7 %copy-start.8 = (f32[3,2304]{1,0:T(4,128)S(1)}, f32[3,2304]{1,0:T(4,128)}, u32[]{:S(2)}) copy-start(f32[3,2304]{1,0:T(4,128)} %copy-done.7) | copy-start | bytes 82948
  80.5 8.9 %copy-start.3 = (f32[6,3,2304]{2,1,0:T(4,128)S(1)}, f32[6,3,2304]{2,1,0:T(4,128)}, u32[]{:S(2)}) copy-start(f32[6,3,2304]{2,1,0:T(4,128)} %param.8) | copy-start | bytes 497668
  80.5 8.8 %copy-start.15 = (f32[3,2256]{1,0:T(4,128)S(1)}, f32[3,2256]{1,0:T(4,128)}, u32[]{:S(2)}) copy-start(f32[3,2256]{1,0:T(4,128)} %get-tuple-element.136) | copy-start | bytes 81220
  80.5 8.8 %copy-start.16 = (f32[3,2256]{1,0:T(4,128)S(1)}, f32[3,2256]{1,0:T(4,128)}, u32[]{:S(2)}) copy-start(f32[3,2256]{1,0:T(4,128)} %get-tuple-element.137) | copy-start | bytes 81220
  80.5 8.8 %copy-start.17 = (f32[3,2256]{1,0:T(4,128)S(1)}, f32[3,2256]{1,0:T(4,128)}, u32[]{:S(2)}) copy-start(f32[3,2256]{1,0:T(4,128)} %get-tuple-element.166) | copy-start | bytes 81220
  80.5 8.8 %copy-start.18 = (f32[3,2256]{1,0:T(4,128)S(1)}, f32[3,2256]{1,0:T(4,128)}, u32[]{:S(2)}) copy-start(f32[3,2256]{1,0:T(4,128)} %get-tuple-element.167) | copy-start | bytes 81220
  80.5 8.8 %copy-start.19 = (f32[3,2256]{1,0:T(4,128)S(1)}, f32[3,2256]{1,0:T(4,128)}, u32[]{:S(2)}) copy-start(f32[3,2256]{1,0:T(4,128)} %get-tuple-element.152) | copy-start | bytes 81220
  81.1 28.0 %collective-permute-start.2 = (bf16[7,27,1,2304]{3,0,2,1:T(8,128)(2,1)S(1)}, bf16[7,27,1,2304]{3,0,2,1:T(8,128)(2,1)S(1)}, u32[]{:S(2)}, u32[]{:S(2)}) collective-permute-start(bf16[7,27,1,2304]{3,0,2,1:T(8,128)(2,1)S(1)} %copy.10), channel_id=1, source_target_pairs={{1,0},{2,1},{3,2},{4,3},{5,4},{6,5},{7,6},{8,7},{9,8},{10,9},{11,1... | collective-permute-start | bytes 2612744 | tf_op jit(solution)/shard_map/ppermute | solution.py:18
  87.1 28.1 %collective-permute-start.1 = (bf16[7,27,1,2304]{3,0,2,1:T(8,128)(2,1)S(1)}, bf16[7,27,1,2304]{3,0,2,1:T(8,128)(2,1)S(1)}, u32[]{:S(2)}, u32[]{:S(2)}) collective-permute-start(bf16[7,27,1,2304]{3,0,2,1:T(8,128)(2,1)S(1)} %copy.9), channel_id=1, source_target_pairs={{0,1},{1,2},{2,3},{3,4},{4,5},{5,6},{6,7},{7,8},{8,9},{9,10},{10,1... | collective-permute-start | bytes 2612744 | tf_op jit(solution)/shard_map/ppermute | solution.py:15
  198.3 25.5 %collective-permute-start.5 = (bf16[7,27,1,2304]{3,0,2,1:T(8,128)(2,1)S(1)}, bf16[7,27,1,2304]{3,0,2,1:T(8,128)(2,1)S(1)}, u32[]{:S(2)}, u32[]{:S(2)}) collective-permute-start(bf16[7,27,1,2304]{3,0,2,1:T(8,128)(2,1)S(1)} %copy.15), channel_id=1, source_target_pairs={{1,0},{2,1},{3,2},{4,3},{5,4},{6,5},{7,6},{8,7},{9,8},{10,9},{11,1... | collective-permute-start | bytes 2612744 | tf_op jit(solution)/shard_map/ppermute | solution.py:18
  200.7 27.6 %collective-permute-start.4 = (bf16[7,27,1,2304]{3,0,2,1:T(8,128)(2,1)S(1)}, bf16[7,27,1,2304]{3,0,2,1:T(8,128)(2,1)S(1)}, u32[]{:S(2)}, u32[]{:S(2)}) collective-permute-start(bf16[7,27,1,2304]{3,0,2,1:T(8,128)(2,1)S(1)} %copy.14), channel_id=1, source_target_pairs={{0,1},{1,2},{2,3},{3,4},{4,5},{5,6},{6,7},{7,8},{8,9},{9,10},{10,1... | collective-permute-start | bytes 2612744 | tf_op jit(solution)/shard_map/ppermute | solution.py:15
  244.4 12.2 %copy-start.1 = (s32[210]{0:T(256)S(1)}, s32[210]{0:T(256)}, u32[]{:S(2)}) copy-start(s32[210]{0:T(256)} %param.11) | copy-start | bytes 2524
  (4 other events, 9.9 us)
